TPU v7x, 512 devices: a whole 4x8x8 slice. The times are simulated.
512 devices in a mesh: src: 16 (over y, x_hi), space: 32 (over x_lo, z, core).
Axes of the slice: x: 4 (x_hi: 2, x_lo: 2; x = x_hi * 2 + x_lo), y: 8, z: 8, core: 2. Of those that a mesh axis runs over, the one named last changes fastest.
Arguments:
- velocity: float32 [32, 512, 256], P('space'), may hold values from 0.5 to 2
- station_cells: int32 [16, 3], P('src'), may hold values from 0 to 511, as said below
- event_cells: int32 [3, 8192], replicated, may hold values from 0 to 511, as said below
- delays: float32 [16, 8192], P('src'), may hold values from -6 to 6
- active: int32 [2, 16, 32, 16], P(None, 'src', 'space'), may hold values from 0 to 1, as said below
Outputs:
- traveltimes: float32 [16, 32, 512, 256], P('src', 'space')
- kernel: float32 [32, 512, 256], P('space', 'src')
Inputs may be any that keep to these rules, and one draw needn't show every extreme that they name: `station_cells`: stations lie in the top four layers: third coordinate below 4, first below 32, second below 512. `event_cells`: row 0 holds first coordinates below 32, row 1 second ones below 512, row 2 third ones below 256. `active`: 1 marks a tile whose cells are updated in that round for that station.
All inputs are finite; a program needn't handle non-finite values.
Results may differ from a plain program's by a relative error of at most 0.0003.
Values sent between devices are 32-bit elements; how exact they have to be, the bound alone decides.
A program may use at most 64 MiB of HBM per device.

v0:
```python
import jax
import jax.numpy as jnp
from jax import lax
from jax.sharding import PartitionSpec as P

TY = 32
ROUNDS = 2
SWEEPS = 2
ADJ_SWEEPS = 4
BIG = 1000000.0


def padded(array, sides, width):
    for axis, dim in sides:
        size, length = (lax.axis_size(axis), array.shape[dim])
        up = [(i, (i + 1) % size) for i in range(size - 1)]
        down = [(j, i) for i, j in up]
        last = lax.slice_in_dim(array, length - width, length, axis=dim)
        first = lax.slice_in_dim(array, 0, width, axis=dim)
        before = lax.ppermute(last, axis, up)
        after = lax.ppermute(first, axis, down)
        array = jnp.concatenate([before, array, after], axis=dim)
    return array


def godunov(near_x, near_y, near_z, cost_cell):
    lowest = jnp.minimum(jnp.minimum(near_x, near_y), near_z)
    highest = jnp.maximum(jnp.maximum(near_x, near_y), near_z)
    middle = jnp.maximum(
        jnp.minimum(near_x, near_y), jnp.minimum(jnp.maximum(near_x, near_y), near_z)
    )
    first_gap = middle - lowest
    second_gap = highest - lowest
    single = lowest + cost_cell
    double = lowest + 0.5 * (
        first_gap + jnp.sqrt(jnp.maximum(2.0 * cost_cell * cost_cell - first_gap * first_gap, 0.0))
    )
    gaps = first_gap + second_gap
    triple = (
        lowest
        + (
            gaps
            + jnp.sqrt(
                jnp.maximum(
                    gaps * gaps
                    - 3.0
                    * (first_gap * first_gap + second_gap * second_gap - cost_cell * cost_cell),
                    0.0,
                )
            )
        )
        / 3.0
    )
    return jnp.where(single <= middle, single, jnp.where(double <= highest, double, triple))


def end_slab(field, axis_index, fill):
    return jnp.full_like(lax.slice_in_dim(field, 0, 1, axis=axis_index), fill)


def shifted(field, axis_index, low_rim, high_rim):
    length = field.shape[axis_index]
    before = jnp.concatenate(
        [low_rim, lax.slice_in_dim(field, 0, length - 1, axis=axis_index)], axis=axis_index
    )
    after = jnp.concatenate(
        [lax.slice_in_dim(field, 1, length, axis=axis_index), high_rim], axis=axis_index
    )
    return (before, after)


def six_neighbours(field, low_rim, high_rim, fill):
    x_before, x_after = shifted(field, 1, low_rim, high_rim)
    y_before, y_after = shifted(field, 2, end_slab(field, 2, fill), end_slab(field, 2, fill))
    z_before, z_after = shifted(field, 3, end_slab(field, 3, fill), end_slab(field, 3, fill))
    return [x_before, x_after, y_before, y_after, z_before, z_after]


def outer_rims(extended):
    position = lax.axis_index("space")
    final_index = lax.axis_size("space") - 1
    low_rim = jnp.where(position == 0, BIG, extended[:, :1])
    high_rim = jnp.where(position == final_index, BIG, extended[:, -1:])
    return (low_rim, high_rim)


def sweep_once(times, slowness, tile_mask, station_mask):
    extended = padded(times, (("space", 1),), 1)
    low_rim, high_rim = outer_rims(extended)
    beside_all = six_neighbours(times, low_rim, high_rim, BIG)
    update = godunov(
        jnp.minimum(beside_all[0], beside_all[1]),
        jnp.minimum(beside_all[2], beside_all[3]),
        jnp.minimum(beside_all[4], beside_all[5]),
        slowness[None],
    )
    station_count, rows_x, rows_y, rows_z = times.shape
    tile_count = rows_y // TY
    shape_tiles = (station_count, rows_x, tile_count, TY, rows_z)
    chosen = jnp.where(tile_mask, update.reshape(shape_tiles), times.reshape(shape_tiles)).reshape(
        times.shape
    )
    return jnp.where(station_mask, 0.0, chosen)


def smooth_along(extended, axis_index):
    length = extended.shape[axis_index]
    first = lax.slice_in_dim(extended, 0, length - 2, axis=axis_index)
    centre = lax.slice_in_dim(extended, 1, length - 1, axis=axis_index)
    after = lax.slice_in_dim(extended, 2, length, axis=axis_index)
    return (first + 2.0 * centre + after) * 0.25


def pad_zero(field, axis_index):
    widths = [(0, 0)] * field.ndim
    widths[axis_index] = (1, 1)
    return jnp.pad(field, widths)


def per_device(velocity, station_cells, event_cells, delays, active):
    slowness = 1.0 / velocity
    rows_x, rows_y, rows_z = velocity.shape
    station_count = station_cells.shape[0]
    offset_x = lax.axis_index("space") * rows_x
    grid_x = (lax.broadcasted_iota(jnp.int32, (rows_x, rows_y, rows_z), 0) + offset_x)[None]
    grid_y = lax.broadcasted_iota(jnp.int32, (rows_x, rows_y, rows_z), 1)[None]
    grid_z = lax.broadcasted_iota(jnp.int32, (rows_x, rows_y, rows_z), 2)[None]
    station_x = station_cells[:, 0][:, None, None, None]
    station_y = station_cells[:, 1][:, None, None, None]
    station_z = station_cells[:, 2][:, None, None, None]
    diff_x = (grid_x - station_x).astype(jnp.float32)
    diff_y = (grid_y - station_y).astype(jnp.float32)
    diff_z = (grid_z - station_z).astype(jnp.float32)
    times = jnp.sqrt(diff_x * diff_x + diff_y * diff_y + diff_z * diff_z)
    station_mask = (grid_x == station_x) & (grid_y == station_y) & (grid_z == station_z)
    for round_index in range(ROUNDS):
        tile_mask = (active[round_index][:, 0, :] > 0)[:, None, :, None, None]
        for sweep in range(SWEEPS):
            times = sweep_once(times, slowness, tile_mask, station_mask)
    cell_count = rows_x * rows_y * rows_z
    event_x = event_cells[0]
    event_y = event_cells[1]
    event_z = event_cells[2]
    local_x = event_x - offset_x
    inside = (local_x >= 0) & (local_x < rows_x)
    flat_index = jnp.where(
        inside, local_x * (rows_y * rows_z) + event_y * rows_z + event_z, cell_count
    )
    flat_times = times.reshape(station_count, cell_count)
    picked = jnp.take(flat_times, jnp.minimum(flat_index, cell_count - 1), axis=1)
    event_dx = (event_x[None, :] - station_cells[:, 0:1]).astype(jnp.float32)
    event_dy = (event_y[None, :] - station_cells[:, 1:2]).astype(jnp.float32)
    event_dz = (event_z[None, :] - station_cells[:, 2:3]).astype(jnp.float32)
    direct = jnp.sqrt(event_dx * event_dx + event_dy * event_dy + event_dz * event_dz)
    misfit = jnp.where(inside[None, :], picked - direct - delays, 0.0)
    source = (
        jnp.zeros((station_count, cell_count), jnp.float32)
        .at[:, flat_index]
        .add(misfit, mode="drop")
    )
    source = source.reshape(times.shape)
    final_ext = padded(times, (("space", 1),), 1)
    low_rim, high_rim = outer_rims(final_ext)
    time_around = six_neighbours(times, low_rim, high_rim, BIG)
    weights = [
        jnp.maximum(neighbour - times, 0.0) * velocity[None] / 6.0 for neighbour in time_around
    ]
    adjoint = source
    for sweep in range(ADJ_SWEEPS):
        adjoint_ext = padded(adjoint, (("space", 1),), 1)
        adjoint_around = six_neighbours(adjoint, adjoint_ext[:, :1], adjoint_ext[:, -1:], 0.0)
        summed = source
        for weight, neighbour in zip(weights, adjoint_around):
            summed = summed + weight * neighbour
        adjoint = summed
    density = slowness * jnp.sum(adjoint, axis=0)
    summed_density = lax.psum(density, "src")
    extended = padded(summed_density, (("space", 0),), 1)
    along_x = smooth_along(extended, 0)
    along_y = smooth_along(pad_zero(along_x, 1), 1)
    filtered = smooth_along(pad_zero(along_y, 2), 2)
    row_count = rows_y // lax.axis_size("src")
    kernel = lax.dynamic_slice_in_dim(filtered, lax.axis_index("src") * row_count, row_count, 1)
    return (times, kernel)


def solution(mesh):
    return jax.shard_map(
        per_device,
        mesh=mesh,
        in_specs=(
            P("space", None, None),
            P("src", None),
            P(),
            P("src", None),
            P(None, "src", "space", None),
        ),
        out_specs=(P("src", "space", None, None), P("space", "src", None)),
        check_vma=False,
    )
```

profile of v0, /device:TPU:2, one launch (start us, length us, event | category | flops | bytes accessed | tf_op | source)
XLA Modules:
  0.0 430.9 jit_solution(12294616544357058122)
XLA Ops:
  10.4 10.4 %collective-permute-start.1 = (f32[1,1,512,256]{3,2,1,0:T(8,128)S(1)}, f32[1,1,512,256]{3,2,1,0:T(8,128)S(1)}, u32[]{:S(2)}, u32[]{:S(2)}) collective-permute-start(f32[1,1,512,256]{3,2,1,0:T(8,128)S(1)} %add_sqrt_fusion), channel_id=1, source_target_pairs={{1,0},{2,1},{3,2},{4,3},{5,4},{6,5},{7,6},{8,7},{9,8},{10,9},{11,1... | collective-permute-start | bytes 1572872 | tf_op jit(solution)/shard_map/ppermute | solution.py:21
  27.5 5.9 %collective-permute-done = f32[1,1,512,256]{3,2,1,0:T(8,128)S(1)} collective-permute-done((f32[1,1,512,256]{3,2,1,0:T(8,128)S(1)}, f32[1,1,512,256]{3,2,1,0:T(8,128)S(1)}, u32[]{:S(2)}, u32[]{:S(2)}) %collective-permute-start) | collective-permute-done | bytes 524320 | tf_op jit(solution)/shard_map/ppermute | solution.py:20
  33.4 2.6 fusion.1
  37.9 2.4 collective-permute-start.2
  40.6 4.0 collective-permute-done.3
  44.6 5.9 %collective-permute-done.2 = f32[1,1,512,256]{3,2,1,0:T(8,128)S(1)} collective-permute-done((f32[1,1,512,256]{3,2,1,0:T(8,128)S(1)}, f32[1,1,512,256]{3,2,1,0:T(8,128)S(1)}, u32[]{:S(2)}, u32[]{:S(2)}) %collective-permute-start.2) | collective-permute-done | bytes 524320 | tf_op jit(solution)/shard_map/ppermute | solution.py:20
  54.7 2.4 collective-permute-start.4
  57.4 4.0 collective-permute-done.5
  61.4 5.9 %collective-permute-done.4 = f32[1,1,512,256]{3,2,1,0:T(8,128)S(1)} collective-permute-done((f32[1,1,512,256]{3,2,1,0:T(8,128)S(1)}, f32[1,1,512,256]{3,2,1,0:T(8,128)S(1)}, u32[]{:S(2)}, u32[]{:S(2)}) %collective-permute-start.4) | collective-permute-done | bytes 524320 | tf_op jit(solution)/shard_map/ppermute | solution.py:20
  71.5 2.4 collective-permute-start.6
  74.2 4.0 collective-permute-done.7
  78.2 5.9 %collective-permute-done.6 = f32[1,1,512,256]{3,2,1,0:T(8,128)S(1)} collective-permute-done((f32[1,1,512,256]{3,2,1,0:T(8,128)S(1)}, f32[1,1,512,256]{3,2,1,0:T(8,128)S(1)}, u32[]{:S(2)}, u32[]{:S(2)}) %collective-permute-start.6) | collective-permute-done | bytes 524320 | tf_op jit(solution)/shard_map/ppermute | solution.py:20
  84.1 2.3 fusion.7
  86.7 45.5 %gather_fusion = f32[8192]{0:T(1024)S(1)} fusion(f32[131072]{0:T(1024)S(1)} %bitcast.79, s32[8192]{0:T(1024)S(1)} %broadcast_clamp_fusion), kind=kCustom, calls=%fused_computation | custom fusion | bytes 98304 | tf_op jit(solution)/shard_map/jit(_take)/gather | solution.py:150
  134.3 43.3 %scatter_custom_fusion = f32[131072]{0:T(1024)S(1)} fusion(s32[8192]{0:T(1024)S(1)} %bitcast.84, f32[8192]{0:T(1024)S(1)} %bitcast.83, f32[]{:T(128)} %constant.24.clone.1), kind=kCustom, calls=%fused_computation.66 | custom fusion | flops 8192 | bytes 524292 | tf_op jit(solution)/shard_map/scatter-add | solution.py:159
  179.8 2.4 collective-permute-start.9
  182.2 5.3 %collective-permute-start.10 = (f32[1,1,512,256]{3,2,1,0:T(8,128)S(1)}, f32[1,1,512,256]{3,2,1,0:T(8,128)S(1)}, u32[]{:S(2)}, u32[]{:S(2)}) collective-permute-start(f32[1,1,512,256]{3,2,1,0:T(8,128)S(1)} %fusion.7), channel_id=1, source_target_pairs={{1,0},{2,1},{3,2},{4,3},{5,4},{6,5},{7,6},{8,7},{9,8},{10,9},{11,1... | collective-permute-start | bytes 1572872 | tf_op jit(solution)/shard_map/ppermute | solution.py:21
  190.1 2.3 collective-permute-done.9
  194.1 5.9 %collective-permute-done.8 = f32[1,1,512,256]{3,2,1,0:T(8,128)S(1)} collective-permute-done((f32[1,1,512,256]{3,2,1,0:T(8,128)S(1)}, f32[1,1,512,256]{3,2,1,0:T(8,128)S(1)}, u32[]{:S(2)}, u32[]{:S(2)}) %collective-permute-start.8) | collective-permute-done | bytes 524320 | tf_op jit(solution)/shard_map/ppermute | solution.py:20
  202.9 2.4 collective-permute-start.12
  205.6 4.0 collective-permute-done.13
  209.6 5.9 %collective-permute-done.12 = f32[1,1,512,256]{3,2,1,0:T(8,128)S(1)} collective-permute-done((f32[1,1,512,256]{3,2,1,0:T(8,128)S(1)}, f32[1,1,512,256]{3,2,1,0:T(8,128)S(1)}, u32[]{:S(2)}, u32[]{:S(2)}) %collective-permute-start.12) | collective-permute-done | bytes 524320 | tf_op jit(solution)/shard_map/ppermute | solution.py:20
  217.9 2.4 collective-permute-start.14
  220.6 4.0 collective-permute-done.15
  224.6 5.9 %collective-permute-done.14 = f32[1,1,512,256]{3,2,1,0:T(8,128)S(1)} collective-permute-done((f32[1,1,512,256]{3,2,1,0:T(8,128)S(1)}, f32[1,1,512,256]{3,2,1,0:T(8,128)S(1)}, u32[]{:S(2)}, u32[]{:S(2)}) %collective-permute-start.14) | collective-permute-done | bytes 524320 | tf_op jit(solution)/shard_map/ppermute | solution.py:20
  232.9 2.4 collective-permute-start.16
  235.6 4.0 collective-permute-done.17
  239.6 5.9 %collective-permute-done.16 = f32[1,1,512,256]{3,2,1,0:T(8,128)S(1)} collective-permute-done((f32[1,1,512,256]{3,2,1,0:T(8,128)S(1)}, f32[1,1,512,256]{3,2,1,0:T(8,128)S(1)}, u32[]{:S(2)}, u32[]{:S(2)}) %collective-permute-start.16) | collective-permute-done | bytes 524320 | tf_op jit(solution)/shard_map/ppermute | solution.py:20
  247.0 159.3 %all-reduce.40.cloned.1.call-done = f32[1,512,256]{2,1,0:T(8,128)} async-done(((f32[1,512,256]{2,1,0:T(8,128)}), f32[1,512,256]{2,1,0:T(8,128)}) %all-reduce.40.cloned.1.call-update) | async-done | bytes 524304 | tf_op jit(solution)/shard_map/psum | solution.py:177
  408.2 2.4 collective-permute-start.18
  410.6 4.6 %collective-permute-done.19 = f32[1,512,256]{2,1,0:T(8,128)S(1)} collective-permute-done((f32[1,512,256]{2,1,0:T(8,128)}, f32[1,512,256]{2,1,0:T(8,128)S(1)}, u32[]{:S(2)}, u32[]{:S(2)}) %collective-permute-start.19) | collective-permute-done | bytes 524320 | tf_op jit(solution)/shard_map/ppermute | solution.py:21
  415.2 6.5 %collective-permute-done.18 = f32[1,512,256]{2,1,0:T(8,128)S(1)} collective-permute-done((f32[1,512,256]{2,1,0:T(8,128)}, f32[1,512,256]{2,1,0:T(8,128)S(1)}, u32[]{:S(2)}, u32[]{:S(2)}) %collective-permute-start.18) | collective-permute-done | bytes 524320 | tf_op jit(solution)/shard_map/ppermute | solution.py:20
  (70 shorter events, 42.6 us)
Async XLA Ops:
  7.2 399.1 %all-reduce.40.cloned.1.call-start = ((), (), s32[]{:S(2)}) async-start(), calls=%async_computation | async-start | bytes 1048576 | tf_op jit(solution)/shard_map/psum | solution.py:177
  7.2 0.7 copy-start.5
  9.1 15.9 %copy-start.3 = (s32[3,8192]{1,0:T(4,128)S(1)}, s32[3,8192]{1,0:T(4,128)}, u32[]{:S(2)}) copy-start(s32[3,8192]{1,0:T(4,128)} %param.7) | copy-start | bytes 294916
  10.4 17.0 %collective-permute-start.1 = (f32[1,1,512,256]{3,2,1,0:T(8,128)S(1)}, f32[1,1,512,256]{3,2,1,0:T(8,128)S(1)}, u32[]{:S(2)}, u32[]{:S(2)}) collective-permute-start(f32[1,1,512,256]{3,2,1,0:T(8,128)S(1)} %add_sqrt_fusion), channel_id=1, source_target_pairs={{1,0},{2,1},{3,2},{4,3},{5,4},{6,5},{7,6},{8,7},{9,8},{10,9},{11,1... | collective-permute-start | bytes 1572872 | tf_op jit(solution)/shard_map/ppermute | solution.py:21
  20.8 12.6 %collective-permute-start = (f32[1,1,512,256]{3,2,1,0:T(8,128)S(1)}, f32[1,1,512,256]{3,2,1,0:T(8,128)S(1)}, u32[]{:S(2)}, u32[]{:S(2)}) collective-permute-start(f32[1,1,512,256]{3,2,1,0:T(8,128)S(1)} %add_sqrt_fusion), channel_id=1, source_target_pairs={{0,1},{1,2},{2,3},{3,4},{4,5},{5,6},{6,7},{7,8},{8,9},{9,10},{10,1... | collective-permute-start | bytes 1572872 | tf_op jit(solution)/shard_map/ppermute | solution.py:20
  23.9 0.7 copy-start.6
  25.4 8.0 %copy-start.1 = (f32[1,512,256]{2,1,0:T(8,128)S(1)}, f32[1,512,256]{2,1,0:T(8,128)}, u32[]{:S(2)}) copy-start(f32[1,512,256]{2,1,0:T(8,128)} %param.5) | copy-start | bytes 1572868
  36.0 8.6 %collective-permute-start.3 = (f32[1,1,512,256]{3,2,1,0:T(8,128)S(1)}, f32[1,1,512,256]{3,2,1,0:T(8,128)S(1)}, u32[]{:S(2)}, u32[]{:S(2)}) collective-permute-start(f32[1,1,512,256]{3,2,1,0:T(8,128)S(1)} %fusion.1), channel_id=1, source_target_pairs={{1,0},{2,1},{3,2},{4,3},{5,4},{6,5},{7,6},{8,7},{9,8},{10,9},{11,1... | collective-permute-start | bytes 1572872 | tf_op jit(solution)/shard_map/ppermute | solution.py:21
  37.9 12.6 %collective-permute-start.2 = (f32[1,1,512,256]{3,2,1,0:T(8,128)S(1)}, f32[1,1,512,256]{3,2,1,0:T(8,128)S(1)}, u32[]{:S(2)}, u32[]{:S(2)}) collective-permute-start(f32[1,1,512,256]{3,2,1,0:T(8,128)S(1)} %fusion.1), channel_id=1, source_target_pairs={{0,1},{1,2},{2,3},{3,4},{4,5},{5,6},{6,7},{7,8},{8,9},{9,10},{10,1... | collective-permute-start | bytes 1572872 | tf_op jit(solution)/shard_map/ppermute | solution.py:20
  52.8 8.6 %collective-permute-start.5 = (f32[1,1,512,256]{3,2,1,0:T(8,128)S(1)}, f32[1,1,512,256]{3,2,1,0:T(8,128)S(1)}, u32[]{:S(2)}, u32[]{:S(2)}) collective-permute-start(f32[1,1,512,256]{3,2,1,0:T(8,128)S(1)} %fusion.3), channel_id=1, source_target_pairs={{1,0},{2,1},{3,2},{4,3},{5,4},{6,5},{7,6},{8,7},{9,8},{10,9},{11,1... | collective-permute-start | bytes 1572872 | tf_op jit(solution)/shard_map/ppermute | solution.py:21
  54.7 12.6 %collective-permute-start.4 = (f32[1,1,512,256]{3,2,1,0:T(8,128)S(1)}, f32[1,1,512,256]{3,2,1,0:T(8,128)S(1)}, u32[]{:S(2)}, u32[]{:S(2)}) collective-permute-start(f32[1,1,512,256]{3,2,1,0:T(8,128)S(1)} %fusion.3), channel_id=1, source_target_pairs={{0,1},{1,2},{2,3},{3,4},{4,5},{5,6},{6,7},{7,8},{8,9},{9,10},{10,1... | collective-permute-start | bytes 1572872 | tf_op jit(solution)/shard_map/ppermute | solution.py:20
  69.6 8.6 %collective-permute-start.7 = (f32[1,1,512,256]{3,2,1,0:T(8,128)S(1)}, f32[1,1,512,256]{3,2,1,0:T(8,128)S(1)}, u32[]{:S(2)}, u32[]{:S(2)}) collective-permute-start(f32[1,1,512,256]{3,2,1,0:T(8,128)S(1)} %fusion.5), channel_id=1, source_target_pairs={{1,0},{2,1},{3,2},{4,3},{5,4},{6,5},{7,6},{8,7},{9,8},{10,9},{11,1... | collective-permute-start | bytes 1572872 | tf_op jit(solution)/shard_map/ppermute | solution.py:21
  71.5 12.6 %collective-permute-start.6 = (f32[1,1,512,256]{3,2,1,0:T(8,128)S(1)}, f32[1,1,512,256]{3,2,1,0:T(8,128)S(1)}, u32[]{:S(2)}, u32[]{:S(2)}) collective-permute-start(f32[1,1,512,256]{3,2,1,0:T(8,128)S(1)} %fusion.5), channel_id=1, source_target_pairs={{0,1},{1,2},{2,3},{3,4},{4,5},{5,6},{6,7},{7,8},{8,9},{9,10},{10,1... | collective-permute-start | bytes 1572872 | tf_op jit(solution)/shard_map/ppermute | solution.py:20
  86.4 113.6 %copy-start = (f32[1,1,512,256]{3,2,1,0:T(8,128)}, f32[1,1,512,256]{3,2,1,0:T(8,128)S(1)}, u32[]{:S(2)}) copy-start(f32[1,1,512,256]{3,2,1,0:T(8,128)S(1)} %fusion.7) | copy-start | bytes 1572868
  86.7 45.6 %copy-start.4 = (f32[1,8192]{1,0:T(1,128)S(1)}, f32[1,8192]{1,0:T(1,128)}, u32[]{:S(2)}) copy-start(f32[1,8192]{1,0:T(1,128)} %param.8) | copy-start | bytes 98308
  177.8 12.3 %collective-permute-start.11 = (f32[1,1,512,256]{3,2,1,0:T(8,128)S(1)}, f32[1,1,512,256]{3,2,1,0:T(8,128)S(1)}, u32[]{:S(2)}, u32[]{:S(2)}) collective-permute-start(f32[1,1,512,256]{3,2,1,0:T(8,128)S(1)} %reshape.397), channel_id=1, source_target_pairs={{1,0},{2,1},{3,2},{4,3},{5,4},{6,5},{7,6},{8,7},{9,8},{10,9},{11,1... | collective-permute-start | bytes 1572872 | tf_op jit(solution)/shard_map/ppermute | solution.py:21
  179.8 12.6 %collective-permute-start.9 = (f32[1,1,512,256]{3,2,1,0:T(8,128)S(1)}, f32[1,1,512,256]{3,2,1,0:T(8,128)S(1)}, u32[]{:S(2)}, u32[]{:S(2)}) collective-permute-start(f32[1,1,512,256]{3,2,1,0:T(8,128)S(1)} %reshape.397), channel_id=1, source_target_pairs={{0,1},{1,2},{2,3},{3,4},{4,5},{5,6},{6,7},{7,8},{8,9},{9,10},{10,1... | collective-permute-start | bytes 1572872 | tf_op jit(solution)/shard_map/ppermute | solution.py:20
  182.2 12.0 %collective-permute-start.10 = (f32[1,1,512,256]{3,2,1,0:T(8,128)S(1)}, f32[1,1,512,256]{3,2,1,0:T(8,128)S(1)}, u32[]{:S(2)}, u32[]{:S(2)}) collective-permute-start(f32[1,1,512,256]{3,2,1,0:T(8,128)S(1)} %fusion.7), channel_id=1, source_target_pairs={{1,0},{2,1},{3,2},{4,3},{5,4},{6,5},{7,6},{8,7},{9,8},{10,9},{11,1... | collective-permute-start | bytes 1572872 | tf_op jit(solution)/shard_map/ppermute | solution.py:21
  187.4 12.6 %collective-permute-start.8 = (f32[1,1,512,256]{3,2,1,0:T(8,128)S(1)}, f32[1,1,512,256]{3,2,1,0:T(8,128)S(1)}, u32[]{:S(2)}, u32[]{:S(2)}) collective-permute-start(f32[1,1,512,256]{3,2,1,0:T(8,128)S(1)} %fusion.7), channel_id=1, source_target_pairs={{0,1},{1,2},{2,3},{3,4},{4,5},{5,6},{6,7},{7,8},{8,9},{9,10},{10,1... | collective-permute-start | bytes 1572872 | tf_op jit(solution)/shard_map/ppermute | solution.py:20
  201.0 8.6 %collective-permute-start.13 = (f32[1,1,512,256]{3,2,1,0:T(8,128)S(1)}, f32[1,1,512,256]{3,2,1,0:T(8,128)S(1)}, u32[]{:S(2)}, u32[]{:S(2)}) collective-permute-start(f32[1,1,512,256]{3,2,1,0:T(8,128)S(1)} %get-tuple-element.4), channel_id=1, source_target_pairs={{1,0},{2,1},{3,2},{4,3},{5,4},{6,5},{7,6},{8,7},{9,8},{10,9},{11,1... | collective-permute-start | bytes 1572872 | tf_op jit(solution)/shard_map/ppermute | solution.py:21
  202.9 12.6 %collective-permute-start.12 = (f32[1,1,512,256]{3,2,1,0:T(8,128)S(1)}, f32[1,1,512,256]{3,2,1,0:T(8,128)S(1)}, u32[]{:S(2)}, u32[]{:S(2)}) collective-permute-start(f32[1,1,512,256]{3,2,1,0:T(8,128)S(1)} %get-tuple-element.4), channel_id=1, source_target_pairs={{0,1},{1,2},{2,3},{3,4},{4,5},{5,6},{6,7},{7,8},{8,9},{9,10},{10,1... | collective-permute-start | bytes 1572872 | tf_op jit(solution)/shard_map/ppermute | solution.py:20
  216.0 8.6 %collective-permute-start.15 = (f32[1,1,512,256]{3,2,1,0:T(8,128)S(1)}, f32[1,1,512,256]{3,2,1,0:T(8,128)S(1)}, u32[]{:S(2)}, u32[]{:S(2)}) collective-permute-start(f32[1,1,512,256]{3,2,1,0:T(8,128)S(1)} %multiply_add_fusion.1), channel_id=1, source_target_pairs={{1,0},{2,1},{3,2},{4,3},{5,4},{6,5},{7,6},{8,7},{9,8},{10,9},{11,1... | collective-permute-start | bytes 1572872 | tf_op jit(solution)/shard_map/ppermute | solution.py:21
  217.9 12.6 %collective-permute-start.14 = (f32[1,1,512,256]{3,2,1,0:T(8,128)S(1)}, f32[1,1,512,256]{3,2,1,0:T(8,128)S(1)}, u32[]{:S(2)}, u32[]{:S(2)}) collective-permute-start(f32[1,1,512,256]{3,2,1,0:T(8,128)S(1)} %multiply_add_fusion.1), channel_id=1, source_target_pairs={{0,1},{1,2},{2,3},{3,4},{4,5},{5,6},{6,7},{7,8},{8,9},{9,10},{10,1... | collective-permute-start | bytes 1572872 | tf_op jit(solution)/shard_map/ppermute | solution.py:20
  231.0 8.6 %collective-permute-start.17 = (f32[1,1,512,256]{3,2,1,0:T(8,128)S(1)}, f32[1,1,512,256]{3,2,1,0:T(8,128)S(1)}, u32[]{:S(2)}, u32[]{:S(2)}) collective-permute-start(f32[1,1,512,256]{3,2,1,0:T(8,128)S(1)} %multiply_add_fusion), channel_id=1, source_target_pairs={{1,0},{2,1},{3,2},{4,3},{5,4},{6,5},{7,6},{8,7},{9,8},{10,9},{11,1... | collective-permute-start | bytes 1572872 | tf_op jit(solution)/shard_map/ppermute | solution.py:21
  232.9 12.6 %collective-permute-start.16 = (f32[1,1,512,256]{3,2,1,0:T(8,128)S(1)}, f32[1,1,512,256]{3,2,1,0:T(8,128)S(1)}, u32[]{:S(2)}, u32[]{:S(2)}) collective-permute-start(f32[1,1,512,256]{3,2,1,0:T(8,128)S(1)} %multiply_add_fusion), channel_id=1, source_target_pairs={{0,1},{1,2},{2,3},{3,4},{4,5},{5,6},{6,7},{7,8},{8,9},{9,10},{10,1... | collective-permute-start | bytes 1572872 | tf_op jit(solution)/shard_map/ppermute | solution.py:20
  406.2 8.9 %collective-permute-start.19 = (f32[1,512,256]{2,1,0:T(8,128)}, f32[1,512,256]{2,1,0:T(8,128)S(1)}, u32[]{:S(2)}, u32[]{:S(2)}) collective-permute-start(f32[1,512,256]{2,1,0:T(8,128)} %all-reduce.40.cloned.1.call-done), channel_id=1, source_target_pairs={{1,0},{2,1},{3,2},{4,3},{5,4},{6,5},{7,6},{8,7},{9,8},{10,9},{11,1... | collective-permute-start | bytes 1572872 | tf_op jit(solution)/shard_map/ppermute | solution.py:21
  408.2 13.5 %collective-permute-start.18 = (f32[1,512,256]{2,1,0:T(8,128)}, f32[1,512,256]{2,1,0:T(8,128)S(1)}, u32[]{:S(2)}, u32[]{:S(2)}) collective-permute-start(f32[1,512,256]{2,1,0:T(8,128)} %all-reduce.40.cloned.1.call-done), channel_id=1, source_target_pairs={{0,1},{1,2},{2,3},{3,4},{4,5},{5,6},{6,7},{7,8},{8,9},{9,10},{10,1... | collective-permute-start | bytes 1572872 | tf_op jit(solution)/shard_map/ppermute | solution.py:20
  410.6 12.2 %copy-start.2 = (f32[1,512,256]{2,1,0:T(8,128)S(1)}, f32[1,512,256]{2,1,0:T(8,128)}, u32[]{:S(2)}) copy-start(f32[1,512,256]{2,1,0:T(8,128)} %all-reduce.40.cloned.1.call-done) | copy-start | bytes 1572868
Sparse Core Ops, SparseCore 0:
  247.1 159.1 all-reduce.39
where the time goes:
time: 432 us; the launch traced here: 431 us
  waiting for transfers between devices  248 us (57%)
  other arithmetic  62.1 us (14%)
  starting transfers between devices  54.3 us (13%)
  local copies, waits for them, and re-layouts  51.1 us (12%)
  between operations  15.7 us (4%)
    psum x1, waiting for transfers between devices, per_device(): summed_density = lax.psum(density, 'src')  159 us
    ppermute x10, waiting for transfers between devices, padded(): before = lax.ppermute(last, axis, up)  56.2 us
    gather x1, local copies, waits for them, and re-layouts, per_device(): jnp.take(flat_times, jnp.minimum(flat_index, cell_count - 1), axis=1)  45.5 us
    scatter-add x1, other arithmetic, per_device(): source = jnp.zeros((station_count, cell_count), jnp.float32).at[:, flat_i...  43.3 us
    ppermute x10, waiting for transfers between devices, padded(): after = lax.ppermute(first, axis, down)  32.1 us
    ppermute x10, starting transfers between devices, padded(): after = lax.ppermute(first, axis, down)  31 us
    ppermute x10, starting transfers between devices, padded(): before = lax.ppermute(last, axis, up)  23.3 us
    select_n x4, other arithmetic, sweep_once(): return jnp.where(station_mask, 0.0, chosen)  9.37 us
  transfers between devices with their start and end apart: 21, of which 20 were waited for; matrix products, arithmetic and copies ran while one was open for 1% of the time, Pallas kernels for 0%

commit v1 on v0

--- a/solution.py
+++ b/solution.py
@@ -174,7 +174,8 @@
             summed = summed + weight * neighbour
         adjoint = summed
     density = slowness * jnp.sum(adjoint, axis=0)
-    summed_density = lax.psum(density, "src")
+    shards = lax.all_gather(density, "src", axis=0, tiled=False)
+    summed_density = shards.sum(axis=0)
     extended = padded(summed_density, (("space", 0),), 1)
     along_x = smooth_along(extended, 0)
     along_y = smooth_along(pad_zero(along_x, 1), 1)

time: 432 us -> 417 us (0.965)
  waiting for transfers between devices: 248 us -> 223 us
  other arithmetic: 62.1 us -> 69 us
    psum x1 -> x0, waiting for transfers between devices: 159 us -> none  [per_device(): summed_density = lax.psum(density, 'src')]
    all_gather x0 -> x1, waiting for transfers between devices: none -> 136 us  [per_device(): shards = lax.all_gather(density, 'src', axis=0, tiled=False)]
where the time goes in v1:
time: 417 us; the launch traced here: 416 us
  waiting for transfers between devices  223 us (53%)
  other arithmetic  69 us (17%)
  starting transfers between devices  57.7 us (14%)
  local copies, waits for them, and re-layouts  50.6 us (12%)
  between operations  15.7 us (4%)
    all_gather x1, waiting for transfers between devices, per_device(): shards = lax.all_gather(density, 'src', axis=0, tiled=False)  136 us
    ppermute x10, waiting for transfers between devices, padded(): before = lax.ppermute(last, axis, up)  55.7 us
    gather x1, local copies, waits for them, and re-layouts, per_device(): jnp.take(flat_times, jnp.minimum(flat_index, cell_count - 1), axis=1)  45.5 us
    scatter-add x1, other arithmetic, per_device(): source = jnp.zeros((station_count, cell_count), jnp.float32).at[:, flat_i...  43.3 us
    ppermute x10, starting transfers between devices, padded(): after = lax.ppermute(first, axis, down)  34.9 us
    ppermute x10, waiting for transfers between devices, padded(): after = lax.ppermute(first, axis, down)  31.2 us
    ppermute x10, starting transfers between devices, padded(): before = lax.ppermute(last, axis, up)  22.8 us
    select_n x4, other arithmetic, sweep_once(): return jnp.where(station_mask, 0.0, chosen)  11.1 us
  transfers between devices with their start and end apart: 21, of which 20 were waited for; matrix products, arithmetic and copies ran while one was open for 1% of the time, Pallas kernels for 0%

profile of v1, /device:TPU:2, one launch (start us, length us, event | category | flops | bytes accessed | tf_op | source)
XLA Modules:
  0.0 416.1 jit_solution(12712590173180804763)
XLA Ops:
  10.8 10.4 %collective-permute-start.1 = (f32[1,1,512,256]{3,2,1,0:T(8,128)S(1)}, f32[1,1,512,256]{3,2,1,0:T(8,128)S(1)}, u32[]{:S(2)}, u32[]{:S(2)}) collective-permute-start(f32[1,1,512,256]{3,2,1,0:T(8,128)S(1)} %add_sqrt_fusion), channel_id=1, source_target_pairs={{1,0},{2,1},{3,2},{4,3},{5,4},{6,5},{7,6},{8,7},{9,8},{10,9},{11,1... | collective-permute-start | bytes 1572872 | tf_op jit(solution)/shard_map/ppermute | solution.py:21
  27.8 5.9 %collective-permute-done = f32[1,1,512,256]{3,2,1,0:T(8,128)S(1)} collective-permute-done((f32[1,1,512,256]{3,2,1,0:T(8,128)S(1)}, f32[1,1,512,256]{3,2,1,0:T(8,128)S(1)}, u32[]{:S(2)}, u32[]{:S(2)}) %collective-permute-start) | collective-permute-done | bytes 524320 | tf_op jit(solution)/shard_map/ppermute | solution.py:20
  33.7 3.7 fusion.1
  39.3 2.4 collective-permute-start.2
  42.0 4.0 collective-permute-done.3
  46.0 5.9 %collective-permute-done.2 = f32[1,1,512,256]{3,2,1,0:T(8,128)S(1)} collective-permute-done((f32[1,1,512,256]{3,2,1,0:T(8,128)S(1)}, f32[1,1,512,256]{3,2,1,0:T(8,128)S(1)}, u32[]{:S(2)}, u32[]{:S(2)}) %collective-permute-start.2) | collective-permute-done | bytes 524320 | tf_op jit(solution)/shard_map/ppermute | solution.py:20
  51.9 2.5 fusion.3
  56.3 2.4 collective-permute-start.4
  59.0 4.0 collective-permute-done.5
  63.0 5.9 %collective-permute-done.4 = f32[1,1,512,256]{3,2,1,0:T(8,128)S(1)} collective-permute-done((f32[1,1,512,256]{3,2,1,0:T(8,128)S(1)}, f32[1,1,512,256]{3,2,1,0:T(8,128)S(1)}, u32[]{:S(2)}, u32[]{:S(2)}) %collective-permute-start.4) | collective-permute-done | bytes 524320 | tf_op jit(solution)/shard_map/ppermute | solution.py:20
  69.0 2.5 fusion.5
  73.4 2.4 collective-permute-start.6
  76.1 4.0 collective-permute-done.7
  80.0 5.9 %collective-permute-done.6 = f32[1,1,512,256]{3,2,1,0:T(8,128)S(1)} collective-permute-done((f32[1,1,512,256]{3,2,1,0:T(8,128)S(1)}, f32[1,1,512,256]{3,2,1,0:T(8,128)S(1)}, u32[]{:S(2)}, u32[]{:S(2)}) %collective-permute-start.6) | collective-permute-done | bytes 524320 | tf_op jit(solution)/shard_map/ppermute | solution.py:20
  86.0 2.5 fusion.7
  88.8 45.5 %gather_fusion = f32[8192]{0:T(1024)S(1)} fusion(f32[131072]{0:T(1024)S(1)} %bitcast.86, s32[8192]{0:T(1024)S(1)} %broadcast_clamp_fusion), kind=kCustom, calls=%fused_computation | custom fusion | bytes 98304 | tf_op jit(solution)/shard_map/jit(_take)/gather | solution.py:150
  136.6 43.3 %scatter_custom_fusion = f32[131072]{0:T(1024)S(1)} fusion(s32[8192]{0:T(1024)S(1)} %bitcast.93, f32[8192]{0:T(1024)S(1)} %bitcast.92, f32[]{:T(128)} %constant.24.clone.1), kind=kCustom, calls=%fused_computation.66 | custom fusion | flops 8192 | bytes 524292 | tf_op jit(solution)/shard_map/scatter-add | solution.py:159
  182.0 2.4 collective-permute-start.9
  184.4 5.3 %collective-permute-start.10 = (f32[1,1,512,256]{3,2,1,0:T(8,128)S(1)}, f32[1,1,512,256]{3,2,1,0:T(8,128)S(1)}, u32[]{:S(2)}, u32[]{:S(2)}) collective-permute-start(f32[1,1,512,256]{3,2,1,0:T(8,128)S(1)} %fusion.7), channel_id=1, source_target_pairs={{1,0},{2,1},{3,2},{4,3},{5,4},{6,5},{7,6},{8,7},{9,8},{10,9},{11,1... | collective-permute-start | bytes 1572872 | tf_op jit(solution)/shard_map/ppermute | solution.py:21
  196.4 5.9 %collective-permute-done.8 = f32[1,1,512,256]{3,2,1,0:T(8,128)S(1)} collective-permute-done((f32[1,1,512,256]{3,2,1,0:T(8,128)S(1)}, f32[1,1,512,256]{3,2,1,0:T(8,128)S(1)}, u32[]{:S(2)}, u32[]{:S(2)}) %collective-permute-start.8) | collective-permute-done | bytes 524320 | tf_op jit(solution)/shard_map/ppermute | solution.py:20
  205.1 2.4 collective-permute-start.12
  207.8 4.0 collective-permute-done.13
  211.8 5.9 %collective-permute-done.12 = f32[1,1,512,256]{3,2,1,0:T(8,128)S(1)} collective-permute-done((f32[1,1,512,256]{3,2,1,0:T(8,128)S(1)}, f32[1,1,512,256]{3,2,1,0:T(8,128)S(1)}, u32[]{:S(2)}, u32[]{:S(2)}) %collective-permute-start.12) | collective-permute-done | bytes 524320 | tf_op jit(solution)/shard_map/ppermute | solution.py:20
  222.9 4.0 collective-permute-done.15
  226.8 5.9 %collective-permute-done.14 = f32[1,1,512,256]{3,2,1,0:T(8,128)S(1)} collective-permute-done((f32[1,1,512,256]{3,2,1,0:T(8,128)S(1)}, f32[1,1,512,256]{3,2,1,0:T(8,128)S(1)}, u32[]{:S(2)}, u32[]{:S(2)}) %collective-permute-start.14) | collective-permute-done | bytes 524320 | tf_op jit(solution)/shard_map/ppermute | solution.py:20
  237.9 4.0 collective-permute-done.17
  241.9 5.9 %collective-permute-done.16 = f32[1,1,512,256]{3,2,1,0:T(8,128)S(1)} collective-permute-done((f32[1,1,512,256]{3,2,1,0:T(8,128)S(1)}, f32[1,1,512,256]{3,2,1,0:T(8,128)S(1)}, u32[]{:S(2)}, u32[]{:S(2)}) %collective-permute-start.16) | collective-permute-done | bytes 524320 | tf_op jit(solution)/shard_map/ppermute | solution.py:20
  249.4 136.2 %all-gather.3.cloned.1.call-done = f32[16,512,256]{2,1,0:T(8,128)} async-done(((f32[1,512,256]{2,1,0:T(8,128)}), f32[16,512,256]{2,1,0:T(8,128)}) %all-gather.3.cloned.1.call-update) | async-done | bytes 8388624 | tf_op jit(solution)/shard_map/all_gather | solution.py:177
  385.5 4.0 reduce.1
  389.5 5.8 %collective-permute-start.19 = (f32[1,512,256]{2,1,0:T(8,128)S(1)}, f32[1,512,256]{2,1,0:T(8,128)S(1)}, u32[]{:S(2)}, u32[]{:S(2)}) collective-permute-start(f32[1,512,256]{2,1,0:T(8,128)S(1)} %bitcast.88), channel_id=1, source_target_pairs={{1,0},{2,1},{3,2},{4,3},{5,4},{6,5},{7,6},{8,7},{9,8},{10,9},{11,1... | collective-permute-start | bytes 1572872 | tf_op jit(solution)/shard_map/ppermute | solution.py:21
  397.3 4.7 %collective-permute-done.19 = f32[1,512,256]{2,1,0:T(8,128)S(1)} collective-permute-done((f32[1,512,256]{2,1,0:T(8,128)S(1)}, f32[1,512,256]{2,1,0:T(8,128)S(1)}, u32[]{:S(2)}, u32[]{:S(2)}) %collective-permute-start.19) | collective-permute-done | bytes 524320 | tf_op jit(solution)/shard_map/ppermute | solution.py:21
  402.0 5.9 %collective-permute-done.18 = f32[1,512,256]{2,1,0:T(8,128)S(1)} collective-permute-done((f32[1,512,256]{2,1,0:T(8,128)S(1)}, f32[1,512,256]{2,1,0:T(8,128)S(1)}, u32[]{:S(2)}, u32[]{:S(2)}) %collective-permute-start.18) | collective-permute-done | bytes 524320 | tf_op jit(solution)/shard_map/ppermute | solution.py:20
  (65 shorter events, 44.8 us)
Async XLA Ops:
  7.2 44.8 %copy-start.1 = (f32[1,512,256]{2,1,0:T(8,128)S(1)}, f32[1,512,256]{2,1,0:T(8,128)}, u32[]{:S(2)}) copy-start(f32[1,512,256]{2,1,0:T(8,128)} %param.5) | copy-start | bytes 1572868
  7.2 378.4 %all-gather.3.cloned.1.call-start = ((), (), s32[]{:S(2)}) async-start(), calls=%async_computation | async-start | bytes 8912896 | tf_op jit(solution)/shard_map/all_gather | solution.py:177
  10.8 17.0 %collective-permute-start.1 = (f32[1,1,512,256]{3,2,1,0:T(8,128)S(1)}, f32[1,1,512,256]{3,2,1,0:T(8,128)S(1)}, u32[]{:S(2)}, u32[]{:S(2)}) collective-permute-start(f32[1,1,512,256]{3,2,1,0:T(8,128)S(1)} %add_sqrt_fusion), channel_id=1, source_target_pairs={{1,0},{2,1},{3,2},{4,3},{5,4},{6,5},{7,6},{8,7},{9,8},{10,9},{11,1... | collective-permute-start | bytes 1572872 | tf_op jit(solution)/shard_map/ppermute | solution.py:21
  21.1 12.6 %collective-permute-start = (f32[1,1,512,256]{3,2,1,0:T(8,128)S(1)}, f32[1,1,512,256]{3,2,1,0:T(8,128)S(1)}, u32[]{:S(2)}, u32[]{:S(2)}) collective-permute-start(f32[1,1,512,256]{3,2,1,0:T(8,128)S(1)} %add_sqrt_fusion), channel_id=1, source_target_pairs={{0,1},{1,2},{2,3},{3,4},{4,5},{5,6},{6,7},{7,8},{8,9},{9,10},{10,1... | collective-permute-start | bytes 1572872 | tf_op jit(solution)/shard_map/ppermute | solution.py:20
  37.4 8.6 %collective-permute-start.3 = (f32[1,1,512,256]{3,2,1,0:T(8,128)S(1)}, f32[1,1,512,256]{3,2,1,0:T(8,128)S(1)}, u32[]{:S(2)}, u32[]{:S(2)}) collective-permute-start(f32[1,1,512,256]{3,2,1,0:T(8,128)S(1)} %fusion.1), channel_id=1, source_target_pairs={{1,0},{2,1},{3,2},{4,3},{5,4},{6,5},{7,6},{8,7},{9,8},{10,9},{11,1... | collective-permute-start | bytes 1572872 | tf_op jit(solution)/shard_map/ppermute | solution.py:21
  39.3 12.6 %collective-permute-start.2 = (f32[1,1,512,256]{3,2,1,0:T(8,128)S(1)}, f32[1,1,512,256]{3,2,1,0:T(8,128)S(1)}, u32[]{:S(2)}, u32[]{:S(2)}) collective-permute-start(f32[1,1,512,256]{3,2,1,0:T(8,128)S(1)} %fusion.1), channel_id=1, source_target_pairs={{0,1},{1,2},{2,3},{3,4},{4,5},{5,6},{6,7},{7,8},{8,9},{9,10},{10,1... | collective-permute-start | bytes 1572872 | tf_op jit(solution)/shard_map/ppermute | solution.py:20
  54.4 8.6 %collective-permute-start.5 = (f32[1,1,512,256]{3,2,1,0:T(8,128)S(1)}, f32[1,1,512,256]{3,2,1,0:T(8,128)S(1)}, u32[]{:S(2)}, u32[]{:S(2)}) collective-permute-start(f32[1,1,512,256]{3,2,1,0:T(8,128)S(1)} %fusion.3), channel_id=1, source_target_pairs={{1,0},{2,1},{3,2},{4,3},{5,4},{6,5},{7,6},{8,7},{9,8},{10,9},{11,1... | collective-permute-start | bytes 1572872 | tf_op jit(solution)/shard_map/ppermute | solution.py:21
  56.3 12.6 %collective-permute-start.4 = (f32[1,1,512,256]{3,2,1,0:T(8,128)S(1)}, f32[1,1,512,256]{3,2,1,0:T(8,128)S(1)}, u32[]{:S(2)}, u32[]{:S(2)}) collective-permute-start(f32[1,1,512,256]{3,2,1,0:T(8,128)S(1)} %fusion.3), channel_id=1, source_target_pairs={{0,1},{1,2},{2,3},{3,4},{4,5},{5,6},{6,7},{7,8},{8,9},{9,10},{10,1... | collective-permute-start | bytes 1572872 | tf_op jit(solution)/shard_map/ppermute | solution.py:20
  71.4 8.6 %collective-permute-start.7 = (f32[1,1,512,256]{3,2,1,0:T(8,128)S(1)}, f32[1,1,512,256]{3,2,1,0:T(8,128)S(1)}, u32[]{:S(2)}, u32[]{:S(2)}) collective-permute-start(f32[1,1,512,256]{3,2,1,0:T(8,128)S(1)} %fusion.5), channel_id=1, source_target_pairs={{1,0},{2,1},{3,2},{4,3},{5,4},{6,5},{7,6},{8,7},{9,8},{10,9},{11,1... | collective-permute-start | bytes 1572872 | tf_op jit(solution)/shard_map/ppermute | solution.py:21
  73.4 12.6 %collective-permute-start.6 = (f32[1,1,512,256]{3,2,1,0:T(8,128)S(1)}, f32[1,1,512,256]{3,2,1,0:T(8,128)S(1)}, u32[]{:S(2)}, u32[]{:S(2)}) collective-permute-start(f32[1,1,512,256]{3,2,1,0:T(8,128)S(1)} %fusion.5), channel_id=1, source_target_pairs={{0,1},{1,2},{2,3},{3,4},{4,5},{5,6},{6,7},{7,8},{8,9},{9,10},{10,1... | collective-permute-start | bytes 1572872 | tf_op jit(solution)/shard_map/ppermute | solution.py:20
  88.4 113.9 %copy-start = (f32[1,1,512,256]{3,2,1,0:T(8,128)}, f32[1,1,512,256]{3,2,1,0:T(8,128)S(1)}, u32[]{:S(2)}) copy-start(f32[1,1,512,256]{3,2,1,0:T(8,128)S(1)} %fusion.7) | copy-start | bytes 1572868
  88.7 45.6 %copy-start.2 = (s32[3,8192]{1,0:T(4,128)S(1)}, s32[3,8192]{1,0:T(4,128)}, u32[]{:S(2)}) copy-start(s32[3,8192]{1,0:T(4,128)} %param.7) | copy-start | bytes 294916
  88.8 45.6 %copy-start.3 = (f32[1,8192]{1,0:T(1,128)S(1)}, f32[1,8192]{1,0:T(1,128)}, u32[]{:S(2)}) copy-start(f32[1,8192]{1,0:T(1,128)} %param.8) | copy-start | bytes 98308
  180.1 12.3 %collective-permute-start.11 = (f32[1,1,512,256]{3,2,1,0:T(8,128)S(1)}, f32[1,1,512,256]{3,2,1,0:T(8,128)S(1)}, u32[]{:S(2)}, u32[]{:S(2)}) collective-permute-start(f32[1,1,512,256]{3,2,1,0:T(8,128)S(1)} %reshape.406), channel_id=1, source_target_pairs={{1,0},{2,1},{3,2},{4,3},{5,4},{6,5},{7,6},{8,7},{9,8},{10,9},{11,1... | collective-permute-start | bytes 1572872 | tf_op jit(solution)/shard_map/ppermute | solution.py:21
  182.0 12.6 %collective-permute-start.9 = (f32[1,1,512,256]{3,2,1,0:T(8,128)S(1)}, f32[1,1,512,256]{3,2,1,0:T(8,128)S(1)}, u32[]{:S(2)}, u32[]{:S(2)}) collective-permute-start(f32[1,1,512,256]{3,2,1,0:T(8,128)S(1)} %reshape.406), channel_id=1, source_target_pairs={{0,1},{1,2},{2,3},{3,4},{4,5},{5,6},{6,7},{7,8},{8,9},{9,10},{10,1... | collective-permute-start | bytes 1572872 | tf_op jit(solution)/shard_map/ppermute | solution.py:20
  184.4 12.0 %collective-permute-start.10 = (f32[1,1,512,256]{3,2,1,0:T(8,128)S(1)}, f32[1,1,512,256]{3,2,1,0:T(8,128)S(1)}, u32[]{:S(2)}, u32[]{:S(2)}) collective-permute-start(f32[1,1,512,256]{3,2,1,0:T(8,128)S(1)} %fusion.7), channel_id=1, source_target_pairs={{1,0},{2,1},{3,2},{4,3},{5,4},{6,5},{7,6},{8,7},{9,8},{10,9},{11,1... | collective-permute-start | bytes 1572872 | tf_op jit(solution)/shard_map/ppermute | solution.py:21
  189.7 12.6 %collective-permute-start.8 = (f32[1,1,512,256]{3,2,1,0:T(8,128)S(1)}, f32[1,1,512,256]{3,2,1,0:T(8,128)S(1)}, u32[]{:S(2)}, u32[]{:S(2)}) collective-permute-start(f32[1,1,512,256]{3,2,1,0:T(8,128)S(1)} %fusion.7), channel_id=1, source_target_pairs={{0,1},{1,2},{2,3},{3,4},{4,5},{5,6},{6,7},{7,8},{8,9},{9,10},{10,1... | collective-permute-start | bytes 1572872 | tf_op jit(solution)/shard_map/ppermute | solution.py:20
  203.2 8.6 %collective-permute-start.13 = (f32[1,1,512,256]{3,2,1,0:T(8,128)S(1)}, f32[1,1,512,256]{3,2,1,0:T(8,128)S(1)}, u32[]{:S(2)}, u32[]{:S(2)}) collective-permute-start(f32[1,1,512,256]{3,2,1,0:T(8,128)S(1)} %get-tuple-element.4), channel_id=1, source_target_pairs={{1,0},{2,1},{3,2},{4,3},{5,4},{6,5},{7,6},{8,7},{9,8},{10,9},{11,1... | collective-permute-start | bytes 1572872 | tf_op jit(solution)/shard_map/ppermute | solution.py:21
  205.1 12.6 %collective-permute-start.12 = (f32[1,1,512,256]{3,2,1,0:T(8,128)S(1)}, f32[1,1,512,256]{3,2,1,0:T(8,128)S(1)}, u32[]{:S(2)}, u32[]{:S(2)}) collective-permute-start(f32[1,1,512,256]{3,2,1,0:T(8,128)S(1)} %get-tuple-element.4), channel_id=1, source_target_pairs={{0,1},{1,2},{2,3},{3,4},{4,5},{5,6},{6,7},{7,8},{8,9},{9,10},{10,1... | collective-permute-start | bytes 1572872 | tf_op jit(solution)/shard_map/ppermute | solution.py:20
  218.2 8.6 %collective-permute-start.15 = (f32[1,1,512,256]{3,2,1,0:T(8,128)S(1)}, f32[1,1,512,256]{3,2,1,0:T(8,128)S(1)}, u32[]{:S(2)}, u32[]{:S(2)}) collective-permute-start(f32[1,1,512,256]{3,2,1,0:T(8,128)S(1)} %multiply_add_fusion.1), channel_id=1, source_target_pairs={{1,0},{2,1},{3,2},{4,3},{5,4},{6,5},{7,6},{8,7},{9,8},{10,9},{11,1... | collective-permute-start | bytes 1572872 | tf_op jit(solution)/shard_map/ppermute | solution.py:21
  220.2 12.6 %collective-permute-start.14 = (f32[1,1,512,256]{3,2,1,0:T(8,128)S(1)}, f32[1,1,512,256]{3,2,1,0:T(8,128)S(1)}, u32[]{:S(2)}, u32[]{:S(2)}) collective-permute-start(f32[1,1,512,256]{3,2,1,0:T(8,128)S(1)} %multiply_add_fusion.1), channel_id=1, source_target_pairs={{0,1},{1,2},{2,3},{3,4},{4,5},{5,6},{6,7},{7,8},{8,9},{9,10},{10,1... | collective-permute-start | bytes 1572872 | tf_op jit(solution)/shard_map/ppermute | solution.py:20
  233.3 8.6 %collective-permute-start.17 = (f32[1,1,512,256]{3,2,1,0:T(8,128)S(1)}, f32[1,1,512,256]{3,2,1,0:T(8,128)S(1)}, u32[]{:S(2)}, u32[]{:S(2)}) collective-permute-start(f32[1,1,512,256]{3,2,1,0:T(8,128)S(1)} %multiply_add_fusion), channel_id=1, source_target_pairs={{1,0},{2,1},{3,2},{4,3},{5,4},{6,5},{7,6},{8,7},{9,8},{10,9},{11,1... | collective-permute-start | bytes 1572872 | tf_op jit(solution)/shard_map/ppermute | solution.py:21
  235.2 12.6 %collective-permute-start.16 = (f32[1,1,512,256]{3,2,1,0:T(8,128)S(1)}, f32[1,1,512,256]{3,2,1,0:T(8,128)S(1)}, u32[]{:S(2)}, u32[]{:S(2)}) collective-permute-start(f32[1,1,512,256]{3,2,1,0:T(8,128)S(1)} %multiply_add_fusion), channel_id=1, source_target_pairs={{0,1},{1,2},{2,3},{3,4},{4,5},{5,6},{6,7},{7,8},{8,9},{9,10},{10,1... | collective-permute-start | bytes 1572872 | tf_op jit(solution)/shard_map/ppermute | solution.py:20
  389.5 12.5 %collective-permute-start.19 = (f32[1,512,256]{2,1,0:T(8,128)S(1)}, f32[1,512,256]{2,1,0:T(8,128)S(1)}, u32[]{:S(2)}, u32[]{:S(2)}) collective-permute-start(f32[1,512,256]{2,1,0:T(8,128)S(1)} %bitcast.88), channel_id=1, source_target_pairs={{1,0},{2,1},{3,2},{4,3},{5,4},{6,5},{7,6},{8,7},{9,8},{10,9},{11,1... | collective-permute-start | bytes 1572872 | tf_op jit(solution)/shard_map/ppermute | solution.py:21
  395.3 12.6 %collective-permute-start.18 = (f32[1,512,256]{2,1,0:T(8,128)S(1)}, f32[1,512,256]{2,1,0:T(8,128)S(1)}, u32[]{:S(2)}, u32[]{:S(2)}) collective-permute-start(f32[1,512,256]{2,1,0:T(8,128)S(1)} %bitcast.89), channel_id=1, source_target_pairs={{0,1},{1,2},{2,3},{3,4},{4,5},{5,6},{6,7},{7,8},{8,9},{9,10},{10,1... | collective-permute-start | bytes 1572872 | tf_op jit(solution)/shard_map/ppermute | solution.py:20
Sparse Core Ops, SparseCore 0:
  249.5 136.0 all-gather.2
